TPU v7x, 32 devices: a whole 2x2x4 slice. The times are simulated.
32 devices in a mesh: replica: 8 (over z, core), group: 4 (over y, x).
Axes of the slice: x: 2, y: 2, z: 4, core: 2. Of those that a mesh axis runs over, the one named last changes fastest.
Arguments:
- tokens: bfloat16 [4096, 2048], P(('replica', 'group')), may hold values from -6 to 6
- lengths: int32 [8], P('replica'), may hold values from 128 to 512, as said below
- exit_layers: int32 [4096], P(('replica', 'group')), may hold values from 7 to 20, as said below
- pre_gain: bfloat16 [2048], P('group'), may hold values from 0.099609375 to 1.8984375
- pre_shift: bfloat16 [2048], P('group'), may hold values from -3 to 3
- query_weight: bfloat16 [2048, 2048], P('group'), may hold values from -0.1875 to 0.1875
- query_bias: bfloat16 [2048], P('group'), may hold values from -3 to 3
- key_weight: bfloat16 [2048, 2048], P('group'), may hold values from -0.1875 to 0.1875
- value_weight: bfloat16 [2048, 2048], P('group'), may hold values from -0.125 to 0.125
- value_bias: bfloat16 [2048], P('group'), may hold values from -3 to 3
- out_weight: bfloat16 [2048, 2048], P('group'), may hold values from -0.5 to 0.5
- out_bias: bfloat16 [2048], P('group'), may hold values from -1.75 to 1.75
- mid_gain: bfloat16 [2048], P('group'), may hold values from 0.099609375 to 1.8984375
- mid_shift: bfloat16 [2048], P('group'), may hold values from -3 to 3
- up_weight: bfloat16 [2048, 8192], P(None, 'group'), may hold values from -0.125 to 0.125
- up_bias: bfloat16 [8192], P('group'), may hold values from -3 to 3
- down_weight: bfloat16 [8192, 2048], P('group'), may hold values from -0.0625 to 0.0625
- down_bias: bfloat16 [2048], P('group'), may hold values from -1.75 to 1.75
- cotangent: bfloat16 [4096, 2048], P(('replica', 'group')), may hold values from -6 to 6
Outputs:
- output: bfloat16 [4096, 2048], P(('replica', 'group'))
- token_grad: bfloat16 [4096, 2048], P(('replica', 'group'))
- pre_gain_grad: float32 [2048], P('group')
- pre_shift_grad: float32 [2048], P('group')
- query_weight_grad: float32 [2048, 2048], P('group')
- query_bias_grad: float32 [2048], P('group')
- key_weight_grad: float32 [2048, 2048], P('group')
- value_weight_grad: float32 [2048, 2048], P('group')
- value_bias_grad: float32 [2048], P('group')
- out_weight_grad: float32 [2048, 2048], P('group')
- out_bias_grad: float32 [2048], P('group')
- mid_gain_grad: float32 [2048], P('group')
- mid_shift_grad: float32 [2048], P('group')
- up_weight_grad: float32 [2048, 8192], P(None, 'group')
- up_bias_grad: float32 [8192], P('group')
- down_weight_grad: float32 [8192, 2048], P('group')
- down_bias_grad: float32 [2048], P('group')
Inputs may be any that keep to these rules, and one draw needn't show every extreme that they name: `lengths`: some sequence has length 512 and some other has length 128. Within each sequence, exit_layers never rise from one position to the next.
All inputs are finite; a program needn't handle non-finite values.
Results may differ from a plain program's by a relative error of at most 0.02.
Values may be sent and summed in bfloat16 or wider, within the bound.
No kernel may reach another device: no remote copies, remote signals or barrier semaphores. Data moves between devices by JAX's collectives and lax.ppermute only.
A program may use at most 640 MiB of HBM per device.

v0:
```python
import jax
import jax.numpy as jnp
from jax import lax
from jax.sharding import PartitionSpec as P

D = 2048
H = 32
HD = 64
LAYER = 12


def layer_norm(values):
    center = values - jnp.mean(values, -1, keepdims=True)
    spread = jnp.mean(center * center, -1, keepdims=True)
    factor = lax.rsqrt(spread + 1e-05)
    return (center * factor, factor)


def norm_back(grad, normal, factor):
    return factor * (
        grad
        - jnp.mean(grad, -1, keepdims=True)
        - normal * jnp.mean(grad * normal, -1, keepdims=True)
    )


def gelu(values):
    return (
        0.5
        * values
        * (1.0 + jnp.tanh(0.7978845608 * (values + 0.044715 * values * values * values)))
    )


def gelu_back(values, grad):
    inner = 0.7978845608 * (values + 0.044715 * values * values * values)
    tangent = jnp.tanh(inner)
    slope = 0.5 * (1.0 + tangent) + 0.5 * values * (1.0 - tangent * tangent) * 0.7978845608 * (
        1.0 + 3.0 * 0.044715 * values * values
    )
    return grad * slope


def split_heads(matrix):
    groups = max(1, H // 8)
    return matrix.reshape(matrix.shape[0], groups, H // groups, HD).transpose(1, 0, 2, 3)


def join_heads(heads):
    return heads.transpose(1, 0, 2, 3).reshape(heads.shape[1], D)


def score_block(query_group, key_group, allowed):
    scores = (
        jnp.einsum("qhd,khd->hqk", query_group, key_group, preferred_element_type=jnp.float32)
        * 0.125
    )
    return jnp.where(allowed[None], scores, -1e30)


def matmul(left, right):
    return jnp.dot(left, right, preferred_element_type=jnp.float32)


def column_sums(matrix):
    return jnp.sum(matrix.astype(jnp.float32), 0)


def shards(
    tokens,
    lengths,
    exit_layers,
    pre_gain,
    pre_shift,
    query_weight,
    query_bias,
    key_weight,
    value_weight,
    value_bias,
    out_weight,
    out_bias,
    mid_gain,
    mid_shift,
    up_weight,
    up_bias,
    down_weight,
    down_bias,
    cotangent,
):
    local_rows = tokens.shape[0]
    group_count = lax.axis_size("group")
    seq_rows = local_rows * group_count
    member = lax.axis_index("group")
    position = member * local_rows + jnp.arange(local_rows, dtype=jnp.int32)
    active = ((position < lengths[0]) & (exit_layers > LAYER)).astype(jnp.float32)[:, None]
    allowed = jnp.arange(seq_rows, dtype=jnp.int32)[None, :] <= position[:, None]
    (
        gain_one,
        shift_one,
        gain_two,
        shift_two,
        query_full,
        key_full,
        value_full,
        out_full,
        qbias_full,
        vbias_full,
        obias_full,
    ) = (
        lax.all_gather(pre_gain, "group", axis=0, tiled=True),
        lax.all_gather(pre_shift, "group", axis=0, tiled=True),
        lax.all_gather(mid_gain, "group", axis=0, tiled=True),
        lax.all_gather(mid_shift, "group", axis=0, tiled=True),
        lax.all_gather(query_weight, "group", axis=0, tiled=True),
        lax.all_gather(key_weight, "group", axis=0, tiled=True),
        lax.all_gather(value_weight, "group", axis=0, tiled=True),
        lax.all_gather(out_weight, "group", axis=0, tiled=True),
        lax.all_gather(query_bias, "group", axis=0, tiled=True),
        lax.all_gather(value_bias, "group", axis=0, tiled=True),
        lax.all_gather(out_bias, "group", axis=0, tiled=True),
    )
    inputs = tokens.astype(jnp.float32)
    normed_one, factor_one = layer_norm(inputs)
    attn_in = (normed_one * gain_one.astype(jnp.float32) + shift_one.astype(jnp.float32)).astype(
        jnp.bfloat16
    )
    queries = (matmul(attn_in, query_full) + qbias_full.astype(jnp.float32)).astype(jnp.bfloat16)
    keys_local = matmul(attn_in, key_full).astype(jnp.bfloat16)
    values_local = (matmul(attn_in, value_full) + vbias_full.astype(jnp.float32)).astype(
        jnp.bfloat16
    )
    keys_all, values_all = (
        lax.all_gather(keys_local, "group", axis=0, tiled=True),
        lax.all_gather(values_local, "group", axis=0, tiled=True),
    )
    query_heads = split_heads(queries)
    key_heads = split_heads(keys_all)
    value_heads = split_heads(values_all)

    def forward_group(operands):
        query_group, key_group, value_group = operands
        scores = score_block(query_group, key_group, allowed)
        top = jnp.max(scores, -1, keepdims=True)
        logsum = top + jnp.log(jnp.sum(jnp.exp(scores - top), -1, keepdims=True))
        weights = jnp.exp(scores - logsum).astype(jnp.bfloat16)
        context_part = jnp.einsum(
            "hqk,khd->qhd", weights, value_group, preferred_element_type=jnp.float32
        )
        return (context_part, logsum[..., 0])

    context_heads, logsums = lax.map(forward_group, (query_heads, key_heads, value_heads))
    context_low = join_heads(context_heads).astype(jnp.bfloat16)
    attn_out = matmul(context_low, out_full) + obias_full.astype(jnp.float32)
    hidden = inputs + active * attn_out
    normed_two, factor_two = layer_norm(hidden)
    ffn_in = (normed_two * gain_two.astype(jnp.float32) + shift_two.astype(jnp.float32)).astype(
        jnp.bfloat16
    )
    up_full, upbias_full, down_full, downbias_full = (
        lax.all_gather(up_weight, "group", axis=1, tiled=True),
        lax.all_gather(up_bias, "group", axis=0, tiled=True),
        lax.all_gather(down_weight, "group", axis=0, tiled=True),
        lax.all_gather(down_bias, "group", axis=0, tiled=True),
    )
    pre_act = matmul(ffn_in, up_full) + upbias_full.astype(jnp.float32)
    act_low = gelu(pre_act).astype(jnp.bfloat16)
    branch = matmul(act_low, down_full) + downbias_full.astype(jnp.float32)
    output = (hidden + active * branch).astype(jnp.bfloat16)
    first_gain, second_gain, query_back, key_back, value_back, out_back = (
        lax.all_gather(pre_gain, "group", axis=0, tiled=True),
        lax.all_gather(mid_gain, "group", axis=0, tiled=True),
        lax.all_gather(query_weight, "group", axis=0, tiled=True),
        lax.all_gather(key_weight, "group", axis=0, tiled=True),
        lax.all_gather(value_weight, "group", axis=0, tiled=True),
        lax.all_gather(out_weight, "group", axis=0, tiled=True),
    )
    grad_out = cotangent.astype(jnp.float32)
    branch_grad = (active * grad_out).astype(jnp.bfloat16)
    up_back, down_back = (
        lax.all_gather(up_weight, "group", axis=1, tiled=True),
        lax.all_gather(down_weight, "group", axis=0, tiled=True),
    )
    act_grad = matmul(branch_grad, down_back.T)
    pre_grad = gelu_back(pre_act, act_grad).astype(jnp.bfloat16)
    ffn_in_grad = matmul(pre_grad, up_back.T)
    up_grad, up_bias_grad, down_grad, down_bias_grad = (
        lax.psum_scatter(
            matmul(ffn_in.T, pre_grad).astype(jnp.bfloat16),
            "group",
            scatter_dimension=1,
            tiled=True,
        ).astype(jnp.float32),
        lax.psum_scatter(
            column_sums(pre_grad).astype(jnp.bfloat16), "group", scatter_dimension=0, tiled=True
        ).astype(jnp.float32),
        lax.psum_scatter(
            matmul(act_low.T, branch_grad).astype(jnp.bfloat16),
            "group",
            scatter_dimension=0,
            tiled=True,
        ).astype(jnp.float32),
        lax.psum_scatter(
            column_sums(branch_grad).astype(jnp.bfloat16), "group", scatter_dimension=0, tiled=True
        ).astype(jnp.float32),
    )
    mid_gain_part = jnp.sum(ffn_in_grad * normed_two, 0)
    mid_shift_part = jnp.sum(ffn_in_grad, 0)
    hidden_grad = grad_out + norm_back(
        ffn_in_grad * second_gain.astype(jnp.float32), normed_two, factor_two
    )
    attn_grad = (active * hidden_grad).astype(jnp.bfloat16)
    context_grad = matmul(attn_grad, out_back.T).astype(jnp.bfloat16)
    out_bias_part = column_sums(attn_grad)

    def backward_group(operands):
        query_group, key_group, value_group, grad_group, logsum_group = operands
        scores = score_block(query_group, key_group, allowed)
        probs = jnp.exp(scores - logsum_group[..., None])
        probs_grad = jnp.einsum(
            "qhd,khd->hqk", grad_group, value_group, preferred_element_type=jnp.float32
        )
        delta = jnp.sum(probs * probs_grad, -1, keepdims=True)
        score_grad = (probs * (probs_grad - delta)).astype(jnp.bfloat16)
        query_part = (
            jnp.einsum("hqk,khd->qhd", score_grad, key_group, preferred_element_type=jnp.float32)
            * 0.125
        )
        key_part = (
            jnp.einsum("hqk,qhd->khd", score_grad, query_group, preferred_element_type=jnp.float32)
            * 0.125
        )
        value_part = jnp.einsum(
            "hqk,qhd->khd",
            probs.astype(jnp.bfloat16),
            grad_group,
            preferred_element_type=jnp.float32,
        )
        return (query_part, key_part, value_part)

    query_parts, key_parts, value_parts = lax.map(
        backward_group, (query_heads, key_heads, value_heads, split_heads(context_grad), logsums)
    )
    query_grad = join_heads(query_parts).astype(jnp.bfloat16)
    key_sum, value_sum = (
        lax.psum_scatter(
            join_heads(key_parts).astype(jnp.bfloat16), "group", scatter_dimension=0, tiled=True
        ).astype(jnp.float32),
        lax.psum_scatter(
            join_heads(value_parts).astype(jnp.bfloat16), "group", scatter_dimension=0, tiled=True
        ).astype(jnp.float32),
    )
    key_grad = key_sum.astype(jnp.bfloat16)
    value_grad = value_sum.astype(jnp.bfloat16)
    in_grad = (
        matmul(query_grad, query_back.T)
        + matmul(key_grad, key_back.T)
        + matmul(value_grad, value_back.T)
    )
    pre_gain_part = jnp.sum(in_grad * normed_one, 0)
    pre_shift_part = jnp.sum(in_grad, 0)
    token_grad = (
        hidden_grad + norm_back(in_grad * first_gain.astype(jnp.float32), normed_one, factor_one)
    ).astype(jnp.bfloat16)
    (
        pre_gain_grad,
        pre_shift_grad,
        mid_gain_grad,
        mid_shift_grad,
        query_wgrad,
        key_wgrad,
        value_wgrad,
        out_wgrad,
        query_bgrad,
        value_bgrad,
        out_bgrad,
    ) = (
        lax.psum_scatter(
            pre_gain_part.astype(jnp.bfloat16), "group", scatter_dimension=0, tiled=True
        ).astype(jnp.float32),
        lax.psum_scatter(
            pre_shift_part.astype(jnp.bfloat16), "group", scatter_dimension=0, tiled=True
        ).astype(jnp.float32),
        lax.psum_scatter(
            mid_gain_part.astype(jnp.bfloat16), "group", scatter_dimension=0, tiled=True
        ).astype(jnp.float32),
        lax.psum_scatter(
            mid_shift_part.astype(jnp.bfloat16), "group", scatter_dimension=0, tiled=True
        ).astype(jnp.float32),
        lax.psum_scatter(
            matmul(attn_in.T, query_grad).astype(jnp.bfloat16),
            "group",
            scatter_dimension=0,
            tiled=True,
        ).astype(jnp.float32),
        lax.psum_scatter(
            matmul(attn_in.T, key_grad).astype(jnp.bfloat16),
            "group",
            scatter_dimension=0,
            tiled=True,
        ).astype(jnp.float32),
        lax.psum_scatter(
            matmul(attn_in.T, value_grad).astype(jnp.bfloat16),
            "group",
            scatter_dimension=0,
            tiled=True,
        ).astype(jnp.float32),
        lax.psum_scatter(
            matmul(context_low.T, attn_grad).astype(jnp.bfloat16),
            "group",
            scatter_dimension=0,
            tiled=True,
        ).astype(jnp.float32),
        lax.psum_scatter(
            column_sums(query_grad).astype(jnp.bfloat16), "group", scatter_dimension=0, tiled=True
        ).astype(jnp.float32),
        lax.psum_scatter(
            column_sums(value_grad).astype(jnp.bfloat16), "group", scatter_dimension=0, tiled=True
        ).astype(jnp.float32),
        lax.psum_scatter(
            out_bias_part.astype(jnp.bfloat16), "group", scatter_dimension=0, tiled=True
        ).astype(jnp.float32),
    )
    totals = (
        lax.psum(pre_gain_grad.astype(jnp.bfloat16), "replica").astype(jnp.float32),
        lax.psum(pre_shift_grad.astype(jnp.bfloat16), "replica").astype(jnp.float32),
        lax.psum(query_wgrad.astype(jnp.bfloat16), "replica").astype(jnp.float32),
        lax.psum(query_bgrad.astype(jnp.bfloat16), "replica").astype(jnp.float32),
        lax.psum(key_wgrad.astype(jnp.bfloat16), "replica").astype(jnp.float32),
        lax.psum(value_wgrad.astype(jnp.bfloat16), "replica").astype(jnp.float32),
        lax.psum(value_bgrad.astype(jnp.bfloat16), "replica").astype(jnp.float32),
        lax.psum(out_wgrad.astype(jnp.bfloat16), "replica").astype(jnp.float32),
        lax.psum(out_bgrad.astype(jnp.bfloat16), "replica").astype(jnp.float32),
        lax.psum(mid_gain_grad.astype(jnp.bfloat16), "replica").astype(jnp.float32),
        lax.psum(mid_shift_grad.astype(jnp.bfloat16), "replica").astype(jnp.float32),
        lax.psum(up_grad.astype(jnp.bfloat16), "replica").astype(jnp.float32),
        lax.psum(up_bias_grad.astype(jnp.bfloat16), "replica").astype(jnp.float32),
        lax.psum(down_grad.astype(jnp.bfloat16), "replica").astype(jnp.float32),
        lax.psum(down_bias_grad.astype(jnp.bfloat16), "replica").astype(jnp.float32),
    )
    return (
        output,
        token_grad,
        totals[0],
        totals[1],
        totals[2],
        totals[3],
        totals[4],
        totals[5],
        totals[6],
        totals[7],
        totals[8],
        totals[9],
        totals[10],
        totals[11],
        totals[12],
        totals[13],
        totals[14],
    )


def solution(mesh):
    return jax.shard_map(
        shards,
        mesh=mesh,
        in_specs=(
            P(("replica", "group"), None),
            P("replica"),
            P(("replica", "group")),
            P("group"),
            P("group"),
            P("group", None),
            P("group"),
            P("group", None),
            P("group", None),
            P("group"),
            P("group", None),
            P("group"),
            P("group"),
            P("group"),
            P(None, "group"),
            P("group"),
            P("group", None),
            P("group"),
            P(("replica", "group"), None),
        ),
        out_specs=(
            P(("replica", "group"), None),
            P(("replica", "group"), None),
            P("group"),
            P("group"),
            P("group", None),
            P("group"),
            P("group", None),
            P("group", None),
            P("group"),
            P("group", None),
            P("group"),
            P("group"),
            P("group"),
            P(None, "group"),
            P("group"),
            P("group", None),
            P("group"),
        ),
        check_vma=False,
    )
```

profile of v0, /device:TPU:0, one launch (start us, length us, event | category | flops | bytes accessed | tf_op | source)
XLA Modules:
  0.0 2687.4 jit_solution(7998907598796842740)
XLA Ops:
  9.5 9.5 all-gather.2
  19.1 8.1 all-gather.1
  27.2 7.1 all-gather
  34.8 65.6 %all-gather.17.cloned.1.call-done = bf16[2048,2048]{1,0:T(8,128)(2,1)} async-done(((bf16[512,2048]{1,0:T(8,128)(2,1)}), bf16[2048,2048]{1,0:T(8,128)(2,1)}) %all-gather.17.cloned.1.call-update) | async-done | bytes 8388624 | tf_op jit(solution)/shard_map/all_gather | solution.py:116
  100.3 5.5 fusion.50
  105.9 83.9 %all-gather.23.cloned.1.call-done = bf16[2048,2048]{1,0:T(8,128)(2,1)} async-done(((bf16[512,2048]{1,0:T(8,128)(2,1)}), bf16[2048,2048]{1,0:T(8,128)(2,1)}) %all-gather.23.cloned.1.call-update) | async-done | bytes 8388624 | tf_op jit(solution)/shard_map/all_gather | solution.py:115
  189.8 5.5 convolution_convert_fusion.7
  197.6 8.0 all-gather.4
  205.7 7.1 all-gather.3
  213.5 8.3 all_gather.73
  221.8 7.1 all-gather.6
  229.0 8.0 all-gather.5
  237.1 42.5 %all-gather.21.cloned.1.call-done = bf16[2048,2048]{1,0:T(8,128)(2,1)} async-done(((bf16[512,2048]{1,0:T(8,128)(2,1)}), bf16[2048,2048]{1,0:T(8,128)(2,1)}) %all-gather.21.cloned.1.call-update) | async-done | bytes 8388624 | tf_op jit(solution)/shard_map/all_gather | solution.py:114
  284.6 32.6 %all-gather.19.cloned.1.call-done = bf16[512,2048]{1,0:T(8,128)(2,1)} async-done(((bf16[128,2048]{1,0:T(8,128)(2,1)}), bf16[512,2048]{1,0:T(8,128)(2,1)}) %all-gather.19.cloned.1.call-update) | async-done | bytes 2097168 | tf_op jit(solution)/shard_map/all_gather | solution.py:134
  321.3 33.5 %all-gather.25.cloned.1.call-done = bf16[512,2048]{1,0:T(8,128)(2,1)} async-done(((bf16[128,2048]{1,0:T(8,128)(2,1)}), bf16[512,2048]{1,0:T(8,128)(2,1)}) %all-gather.25.cloned.1.call-update) | async-done | bytes 2097168 | tf_op jit(solution)/shard_map/all_gather | solution.py:133
  358.6 15.8 while.28
  374.4 69.8 %all-gather.27.cloned.1.call-done = bf16[2048,2048]{1,0:T(8,128)(2,1)} async-done(((bf16[512,2048]{1,0:T(8,128)(2,1)}), bf16[2048,2048]{1,0:T(8,128)(2,1)}) %all-gather.27.cloned.1.call-update) | async-done | bytes 8388624 | tf_op jit(solution)/shard_map/all_gather | solution.py:117
  450.3 292.9 %all-gather.29.cloned.1.call-done = bf16[2048,8192]{1,0:T(8,128)(2,1)} async-done(((bf16[2048,2048]{1,0:T(8,128)(2,1)}), bf16[2048,8192]{1,0:T(8,128)(2,1)}) %all-gather.29.cloned.1.call-update) | async-done | bytes 33554448 | tf_op jit(solution)/shard_map/all_gather | solution.py:160
  743.3 20.8 convolution_add_fusion
  764.0 278.3 %all-gather.31.cloned.1.call-done = bf16[8192,2048]{1,0:T(8,128)(2,1)} async-done(((bf16[2048,2048]{1,0:T(8,128)(2,1)}), bf16[8192,2048]{1,0:T(8,128)(2,1)}) %all-gather.31.cloned.1.call-update) | async-done | bytes 33554448 | tf_op jit(solution)/shard_map/all_gather | solution.py:162
  1042.3 18.8 fusion.81
  1061.2 19.7 multiply_reduce_fusion.1
  1085.0 7.1 convolution_convert_fusion.6
  1095.0 31.3 %while.29 = (s32[]{:T(128)}, bf16[4,128,8,64]{1,3,2,0:T(8,128)(2,1)}, bf16[4,512,8,64]{1,3,2,0:T(8,128)(2,1)}, bf16[4,512,8,64]{1,3,2,0:T(8,128)(2,1)}, bf16[4,5...) while((s32[]{:T(128)}, ...), condition=%wide.region_12.13_spmd.clone, body=%wide.region_10.12_spmd.clone.sunk | while | flops 340655104 | bytes 58091296 | solution.py:240
  1134.3 5.9 convolution_convert_fusion.5
  1141.4 5.5 convolution_convert_fusion.2
  1147.0 18.6 reduce-scatter.25.cloned.1.call-done
  1165.6 6.9 convolution_convert_fusion.4
  1172.5 31.9 %reduce-scatter.27.cloned.1.call-done = bf16[128,2048]{1,0:T(8,128)(2,1)} async-done(((bf16[512,2048]{1,0:T(8,128)(2,1)}), bf16[128,2048]{1,0:T(8,128)(2,1)}) %reduce-scatter.27.cloned.1.call-update) | async-done | bytes 524304
  1204.4 6.8 convolution_convert_fusion.3
  1212.4 15.7 convolution_convert_fusion
  1229.1 16.6 convolution_convert_fusion.1
  1245.8 48.8 %reduce-scatter.15.cloned.1.call-done = bf16[512,2048]{1,0:T(8,128)(2,1)} async-done(((bf16[2048,2048]{1,0:T(8,128)(2,1)}), bf16[512,2048]{1,0:T(8,128)(2,1)}) %reduce-scatter.15.cloned.1.call-update) | async-done | bytes 2097168 | tf_op jit(solution)/shard_map/reduce_scatter | solution.py:289
  1294.5 89.6 %reduce-scatter.21.cloned.1.call-done = bf16[512,2048]{1,0:T(8,128)(2,1)} async-done(((bf16[2048,2048]{1,0:T(8,128)(2,1)}), bf16[512,2048]{1,0:T(8,128)(2,1)}) %reduce-scatter.21.cloned.1.call-update) | async-done | bytes 2097168 | tf_op jit(solution)/shard_map/reduce_scatter | solution.py:307
  1384.2 90.1 %reduce-scatter.17.cloned.1.call-done = bf16[512,2048]{1,0:T(8,128)(2,1)} async-done(((bf16[2048,2048]{1,0:T(8,128)(2,1)}), bf16[512,2048]{1,0:T(8,128)(2,1)}) %reduce-scatter.17.cloned.1.call-update) | async-done | bytes 2097168 | tf_op jit(solution)/shard_map/reduce_scatter | solution.py:295
  1474.2 89.6 %reduce-scatter.19.cloned.1.call-done = bf16[512,2048]{1,0:T(8,128)(2,1)} async-done(((bf16[2048,2048]{1,0:T(8,128)(2,1)}), bf16[512,2048]{1,0:T(8,128)(2,1)}) %reduce-scatter.19.cloned.1.call-update) | async-done | bytes 2097168 | tf_op jit(solution)/shard_map/reduce_scatter | solution.py:301
  1563.9 291.6 %reduce-scatter.23.cloned.1.call-done = bf16[2048,2048]{1,0:T(8,128)(2,1)} async-done(((bf16[2048,8192]{1,0:T(8,128)(2,1)}), bf16[2048,2048]{1,0:T(8,128)(2,1)}) %reduce-scatter.23.cloned.1.call-update) | async-done | bytes 8388624 | tf_op jit(solution)/shard_map/reduce_scatter | solution.py:187
  1855.5 291.9 %reduce-scatter.29.cloned.1.call-done = bf16[2048,2048]{1,0:T(8,128)(2,1)} async-done(((bf16[8192,2048]{1,0:T(8,128)(2,1)}), bf16[2048,2048]{1,0:T(8,128)(2,1)}) %reduce-scatter.29.cloned.1.call-update) | async-done | bytes 8388624
  2148.0 8.1 all-gather.7
  2158.5 6.3 fusion.82
  2164.9 18.0 fusion.52
  2183.0 6.5 convolution_add_fusion.3
  2189.5 6.8 fusion.66
  2196.2 16.3 all-reduce.12
  2213.1 28.0 %all-reduce.10 = (bf16[512]{0:T(512)(128)(2,1)S(1)}, bf16[512]{0:T(512)(128)(2,1)S(1)}, bf16[512]{0:T(512)(128)(2,1)S(1)}, bf16[512]{0:T(512)(128)(2,1)S(1)}, bf...) all-reduce(bf16[512]{0:T(512)(128)(2,1)S(1)} %dynamic-slice.1, ...), channel_id=1, replica_groups=mesh['replica'=8,'group'=4] {'replica'}, use_global_device_ids=true, to_apply=%region_19.20 | all-reduce | flops 6144 | bytes 24576 | tf_op jit(solution)/shard_map/psum | solution.py:324
  2247.6 397.6 %all-reduce.15.cloned.1.call-done = (bf16[512,2048]{1,0:T(8,128)(2,1)}, bf16[512,2048]{1,0:T(8,128)(2,1)}, bf16[512,2048]{1,0:T(8,128)(2,1)}, bf16[512,2048]{1,0...) async-done(((bf16[512,2048]{1,0:T(8,128)(2,1)}, bf16[512,2048]{1,0:T(8,128)(2,1)}, bf16[512,2048]{1,0:T(8,128)(2,1)}, bf16[512,2048]{1,0:T(8,128)(2,1)}, ...) | async-done | bytes 25165840 | tf_op jit(solution)/shard_map/psum | solution.py:326
  2657.1 11.7 convert_element_type.296
  2668.8 11.7 convert_element_type.299
  (268 shorter events, 109.9 us)
Async XLA Ops:
  7.2 2.3 copy-start.22
  7.2 11.9 copy-start.23
  7.2 19.9 copy-start.24
  7.2 27.1 %copy-start = (bf16[128,2048]{1,0:T(8,128)(2,1)S(1)}, bf16[128,2048]{1,0:T(8,128)(2,1)}, u32[]{:S(2)}) copy-start(bf16[128,2048]{1,0:T(8,128)(2,1)} %param.23) | copy-start | bytes 1572868
  7.2 93.1 %all-gather.17.cloned.1.call-start = ((), (), s32[]{:S(2)}) async-start(), calls=%async_computation.8 | async-start | bytes 10485760 | tf_op jit(solution)/shard_map/all_gather | solution.py:116
  8.0 181.9 %all-gather.23.cloned.1.call-start = ((), (), s32[]{:S(2)}) async-start(), calls=%async_computation.11 | async-start | bytes 10485760 | tf_op jit(solution)/shard_map/all_gather | solution.py:115
  8.7 270.9 %all-gather.21.cloned.1.call-start = ((), (), s32[]{:S(2)}) async-start(), calls=%async_computation.10 | async-start | bytes 10485760 | tf_op jit(solution)/shard_map/all_gather | solution.py:114
  9.4 307.7 %all-gather.19.cloned.1.call-start = ((), (), s32[]{:S(2)}) async-start(), calls=%async_computation.9 | async-start | bytes 2621440 | tf_op jit(solution)/shard_map/all_gather | solution.py:134
  105.9 248.9 %all-gather.25.cloned.1.call-start = ((), (), s32[]{:S(2)}) async-start(), calls=%async_computation.12 | async-start | bytes 2621440 | tf_op jit(solution)/shard_map/all_gather | solution.py:133
  195.4 248.8 %all-gather.27.cloned.1.call-start = ((), (), s32[]{:S(2)}) async-start(), calls=%async_computation.13 | async-start | bytes 10485760 | tf_op jit(solution)/shard_map/all_gather | solution.py:117
  195.9 547.3 %all-gather.29.cloned.1.call-start = ((), (), s32[]{:S(2)}) async-start(), calls=%async_computation.14 | async-start | bytes 41943040 | tf_op jit(solution)/shard_map/all_gather | solution.py:160
  196.7 9.0 copy-start.26
  196.7 16.8 copy-start.21
  196.7 25.1 copy-start.27
  196.7 32.2 %copy-start.28 = (bf16[512]{0:T(512)(128)(2,1)S(1)}, bf16[512]{0:T(512)(128)(2,1)}, u32[]{:S(2)}) copy-start(bf16[512]{0:T(512)(128)(2,1)} %param.35) | copy-start | bytes 3076
  196.7 40.3 %copy-start.30 = (s32[128]{0:T(128)S(1)}, s32[128]{0:T(128)}, u32[]{:S(2)}) copy-start(s32[128]{0:T(128)} %param.25) | copy-start | bytes 1540
  196.8 845.6 %all-gather.31.cloned.1.call-start = ((), (), s32[]{:S(2)}) async-start(), calls=%async_computation.15 | async-start | bytes 41943040 | tf_op jit(solution)/shard_map/all_gather | solution.py:162
  197.5 968.0 %reduce-scatter.25.cloned.1.call-start = ((), (), s32[]{:S(2)}) async-start(), calls=%async_computation.21 | async-start | bytes 2621440
  1097.7 1.6 copy-start.17
  1097.7 2.4 copy-start.19
  1098.5 3.0 copy-start.7
  1099.6 1.9 copy-start.18
  1105.5 1.6 copy-start.17
  1105.5 2.4 copy-start.19
  1106.3 3.0 copy-start.7
  1107.4 1.9 copy-start.18
  1113.3 1.6 copy-start.17
  1113.3 2.4 copy-start.19
  1114.1 3.0 copy-start.7
  1115.2 1.9 copy-start.18
  1121.2 2.4 copy-start.19
  1121.9 3.0 copy-start.7
  1123.1 1.9 copy-start.18
  1130.2 4.1 copy-start.8
  1130.2 74.2 %reduce-scatter.27.cloned.1.call-start = ((), (), s32[]{:S(2)}) async-start(), calls=%async_computation.22 | async-start | bytes 2621440
  1134.2 160.3 %reduce-scatter.15.cloned.1.call-start = ((), (), s32[]{:S(2)}) async-start(), calls=%async_computation.16 | async-start | bytes 10485760 | tf_op jit(solution)/shard_map/reduce_scatter | solution.py:289
  1140.2 244.0 %reduce-scatter.21.cloned.1.call-start = ((), (), s32[]{:S(2)}) async-start(), calls=%async_computation.19 | async-start | bytes 10485760 | tf_op jit(solution)/shard_map/reduce_scatter | solution.py:307
  1146.9 327.3 %reduce-scatter.17.cloned.1.call-start = ((), (), s32[]{:S(2)}) async-start(), calls=%async_computation.17 | async-start | bytes 10485760 | tf_op jit(solution)/shard_map/reduce_scatter | solution.py:295
  1172.5 391.4 %reduce-scatter.19.cloned.1.call-start = ((), (), s32[]{:S(2)}) async-start(), calls=%async_computation.18 | async-start | bytes 10485760 | tf_op jit(solution)/shard_map/reduce_scatter | solution.py:301
  1211.2 644.3 %reduce-scatter.23.cloned.1.call-start = ((), (), s32[]{:S(2)}) async-start(), calls=%async_computation.20 | async-start | bytes 41943040 | tf_op jit(solution)/shard_map/reduce_scatter | solution.py:187
  1228.1 919.2 %reduce-scatter.29.cloned.1.call-start = ((), (), s32[]{:S(2)}) async-start(), calls=%async_computation.23 | async-start | bytes 41943040
  1245.7 1399.5 %all-reduce.15.cloned.1.call-start = ((), (), s32[]{:S(2)}) async-start(), calls=%async_computation.24 | async-start | bytes 50331648 | tf_op jit(solution)/shard_map/psum | solution.py:326
  2147.4 8.8 copy-start.31
  2164.8 18.1 copy-start.9
  2189.5 56.9 %copy-start.12 = (f32[128,2048]{1,0:T(8,128)S(1)}, f32[128,2048]{1,0:T(8,128)}, u32[]{:S(2)}) copy-start(f32[128,2048]{1,0:T(8,128)} %get-tuple-element.224) | copy-start | bytes 3145732
  2645.2 4.3 copy-start.16
  2649.5 2.5 copy-start.15
  2652.0 2.5 copy-start.14
  (25 other events, 28.6 us)
Sparse Core Ops, SparseCore 0:
  9.9 90.3 all-gather.16
  102.2 87.5 all-gather.22
  191.7 87.8 all-gather.20
  281.8 35.3 all-gather.18
  319.5 35.2 all-gather.24
  356.5 87.5 all-gather.26
  446.0 297.2 all-gather.28
  745.1 297.2 all-gather.30
  1130.3 35.1 reduce-scatter.24
  1169.2 35.1 reduce-scatter.26
  1208.1 86.3 reduce-scatter.14
  1297.7 86.3 reduce-scatter.20
  1387.8 86.3 reduce-scatter.16
  1477.4 86.3 reduce-scatter.18
  1566.8 288.6 reduce-scatter.22
  1858.7 288.6 reduce-scatter.28
  2150.5 494.6 all-reduce.14
where the time goes:
time: 2690 us
  waiting for transfers between devices  2250 us (84%)
  matrix products  210 us (8%)
  blocking collectives  116 us (4%)
  other arithmetic  50.9 us (2%)
  local copies, waits for them, and re-layouts  39.5 us (1%)
    psum x1, waiting for transfers between devices, shards(): lax.psum(query_wgrad.astype(jnp.bfloat16), 'replica').astype(jnp.float32)  398 us
    unnamed x20, waiting for transfers between devices  346 us
    all_gather x1, waiting for transfers between devices, shards(): lax.all_gather(up_weight, 'group', axis=1, tiled=True)  293 us
    reduce_scatter x1, waiting for transfers between devices, shards(): lax.psum_scatter(matmul(ffn_in.T, pre_grad).astype(jnp.bfloat16), 'group'...  292 us
    all_gather x1, waiting for transfers between devices, shards(): lax.all_gather(down_weight, 'group', axis=0, tiled=True)  278 us
    dot_general x18, matrix products, matmul(): return jnp.dot(left, right, preferred_element_type=jnp.float32)  182 us
    reduce_scatter x1, waiting for transfers between devices, shards(): lax.psum_scatter(matmul(attn_in.T, key_grad).astype(jnp.bfloat16), 'group...  90.1 us
    reduce_scatter x1, waiting for transfers between devices, shards(): lax.psum_scatter(matmul(attn_in.T, value_grad).astype(jnp.bfloat16), 'gro...  89.6 us
  transfers between devices with their start and end apart: 17, of which 17 were waited for; matrix products, arithmetic and copies ran while one was open for 6% of the time, Pallas kernels for 0%

commit v1 on v0

--- a/solution.py
+++ b/solution.py
@@ -1,3 +1,4 @@
+import functools
 import jax
 import jax.numpy as jnp
 from jax import lax
@@ -7,6 +8,25 @@
 H = 32
 HD = 64
 LAYER = 12
+
+
+def seats_all_test(vec, mesh_name):
+    cores_n = jax.lax.psum(1, axis_name=mesh_name)
+    frames = [(at, (at + 1) % cores_n) for at in range(cores_n)]
+    f_now, shaped = ([vec], [vec])
+    pages = [(at, (at - 1) % cores_n) for at in range(cores_n)]
+    for _ in range(cores_n // 2):
+        f_now.append(jax.lax.ppermute(f_now[-1], axis_name=mesh_name, perm=frames))
+    for _ in [*range((cores_n - 1) // 2)]:
+        shaped.append(jax.lax.ppermute(shaped[-1], axis_name=mesh_name, perm=pages))
+    return jnp.roll(
+        jnp.concatenate([*f_now[::-1], *shaped[1:]], axis=0),
+        (jax.lax.axis_index(mesh_name) - cores_n // 2) * vec.shape[0],
+        axis=0,
+    )
+
+
+quotas_take = functools.partial(seats_all_test, mesh_name="group")
 
 
 def layer_norm(values):
@@ -113,7 +133,7 @@
         lax.all_gather(mid_shift, "group", axis=0, tiled=True),
         lax.all_gather(query_weight, "group", axis=0, tiled=True),
         lax.all_gather(key_weight, "group", axis=0, tiled=True),
-        lax.all_gather(value_weight, "group", axis=0, tiled=True),
+        quotas_take(value_weight),
         lax.all_gather(out_weight, "group", axis=0, tiled=True),
         lax.all_gather(query_bias, "group", axis=0, tiled=True),
         lax.all_gather(value_bias, "group", axis=0, tiled=True),

time: 2690 us -> 2840 us (1.056)
  blocking collectives: 116 us -> 236 us
    all_gather x1, blocking collectives: 9.52 us -> 130 us  [shards(): lax.all_gather(value_bias, 'group', axis=0, tiled=True)]
    all_gather x1, waiting for transfers between devices: 83.9 us -> 0.02 us  [shards(): lax.all_gather(key_weight, 'group', axis=0, tiled=True)]
    ppermute x0 -> x3, waiting for transfers between devices: none -> 72.5 us  [the longest x2 72.5 us: seats_all_test(): f_now.append(jax.lax.ppermute(f_now[-1], axis_name=mesh_name, perm=frames))]
    psum x1, waiting for transfers between devices: 398 us -> 440 us  [shards(): lax.psum(query_wgrad.astype(jnp.bfloat16), 'replica').astype(jnp.float32)]
    all_gather x1, waiting for transfers between devices: 32.6 us -> 0.02 us  [shards(): lax.all_gather(values_local, 'group', axis=0, tiled=True)]
    all_gather x1, waiting for transfers between devices: 42.5 us -> 73.2 us  [shards(): lax.all_gather(query_weight, 'group', axis=0, tiled=True)]
  transfers between devices with their start and end apart: 17 -> 20, of which waited for: 17 -> 16; matrix products, arithmetic and copies ran while one was open for 6% -> 6% of each run, Pallas kernels for 0% -> 0%
where the time goes in v1:
time: 2840 us; the launch traced here: 2830 us
  waiting for transfers between devices  2260 us (80%)
  blocking collectives  236 us (8%)
  matrix products  208 us (7%)
  other arithmetic  53 us (2%)
  local copies, waits for them, and re-layouts  50.1 us (2%)
    psum x1, waiting for transfers between devices, shards(): lax.psum(query_wgrad.astype(jnp.bfloat16), 'replica').astype(jnp.float32)  440 us
    unnamed x20, waiting for transfers between devices  346 us
    all_gather x1, waiting for transfers between devices, shards(): lax.all_gather(up_weight, 'group', axis=1, tiled=True)  293 us
    reduce_scatter x1, waiting for transfers between devices, shards(): lax.psum_scatter(matmul(ffn_in.T, pre_grad).astype(jnp.bfloat16), 'group'...  292 us
    all_gather x1, waiting for transfers between devices, shards(): lax.all_gather(down_weight, 'group', axis=0, tiled=True)  278 us
    dot_general x18, matrix products, matmul(): return jnp.dot(left, right, preferred_element_type=jnp.float32)  180 us
    all_gather x1, blocking collectives, shards(): lax.all_gather(value_bias, 'group', axis=0, tiled=True)  130 us
    reduce_scatter x1, waiting for transfers between devices, shards(): lax.psum_scatter(matmul(attn_in.T, key_grad).astype(jnp.bfloat16), 'group...  89.9 us
  transfers between devices with their start and end apart: 20, of which 16 were waited for; matrix products, arithmetic and copies ran while one was open for 6% of the time, Pallas kernels for 0%

profile of v1, /device:TPU:0, one launch (start us, length us, event | category | flops | bytes accessed | tf_op | source)
XLA Modules:
  0.0 2832.2 jit_solution(7306997428938926380)
XLA Ops:
  11.0 72.5 %collective-permute-done = bf16[512,2048]{1,0:T(8,128)(2,1)S(1)} collective-permute-done((bf16[512,2048]{1,0:T(8,128)(2,1)}, bf16[512,2048]{1,0:T(8,128)(2,1)S(1)}, u32[]{:S(2)}, u32[]{:S(2)}) %collective-permute-start) | collective-permute-done | bytes 2097184 | tf_op jit(solution)/shard_map/ppermute | solution.py:19
  87.3 130.2 %all-gather.2 = bf16[4,1,512]{2,1,0:T(2,128)(2,1)S(1)} all-gather(bf16[1,1,512]{2,1,0:T(2,128)(2,1)S(1)} %reshape.148), channel_id=1, replica_groups=mesh['replica'=8,'group'=4] {'group'}, dimensions={0}, use_global_device_ids=true | all-gather | bytes 5120 | tf_op jit(solution)/shard_map/all_gather | solution.py:139
  218.2 8.1 all-gather.1
  227.0 7.0 all-gather
  247.8 5.5 convolution_convert_fusion.7
  255.4 8.1 all-gather.4
  263.6 7.1 all-gather.3
  271.3 8.4 all_gather.71
  279.7 7.1 all-gather.6
  286.8 8.3 all-gather.5
  299.3 73.2 %all-gather.19.cloned.1.call-done = bf16[2048,2048]{1,0:T(8,128)(2,1)} async-done(((bf16[512,2048]{1,0:T(8,128)(2,1)}), bf16[2048,2048]{1,0:T(8,128)(2,1)}) %all-gather.19.cloned.1.call-update) | async-done | bytes 8388624 | tf_op jit(solution)/shard_map/all_gather | solution.py:134
  372.5 4.7 fusion.55
  377.5 32.6 %all-gather.23.cloned.1.call-done = bf16[512,2048]{1,0:T(8,128)(2,1)} async-done(((bf16[128,2048]{1,0:T(8,128)(2,1)}), bf16[512,2048]{1,0:T(8,128)(2,1)}) %all-gather.23.cloned.1.call-update) | async-done | bytes 2097168 | tf_op jit(solution)/shard_map/all_gather | solution.py:153
  413.9 15.8 while.28
  429.7 69.7 %all-gather.25.cloned.1.call-done = bf16[2048,2048]{1,0:T(8,128)(2,1)} async-done(((bf16[512,2048]{1,0:T(8,128)(2,1)}), bf16[2048,2048]{1,0:T(8,128)(2,1)}) %all-gather.25.cloned.1.call-update) | async-done | bytes 8388624 | tf_op jit(solution)/shard_map/all_gather | solution.py:137
  499.5 5.0 fusion.88
  505.8 292.7 %all-gather.27.cloned.1.call-done = bf16[2048,8192]{1,0:T(8,128)(2,1)} async-done(((bf16[2048,2048]{1,0:T(8,128)(2,1)}), bf16[2048,8192]{1,0:T(8,128)(2,1)}) %all-gather.27.cloned.1.call-update) | async-done | bytes 33554448 | tf_op jit(solution)/shard_map/all_gather | solution.py:180
  798.5 20.8 convolution_add_fusion
  819.2 278.3 %all-gather.29.cloned.1.call-done = bf16[8192,2048]{1,0:T(8,128)(2,1)} async-done(((bf16[2048,2048]{1,0:T(8,128)(2,1)}), bf16[8192,2048]{1,0:T(8,128)(2,1)}) %all-gather.29.cloned.1.call-update) | async-done | bytes 33554448 | tf_op jit(solution)/shard_map/all_gather | solution.py:182
  1097.5 19.3 fusion.89
  1116.8 19.3 multiply_reduce_fusion.1
  1140.2 7.1 convolution_convert_fusion.6
  1150.3 31.3 %while.29 = (s32[]{:T(128)}, bf16[4,128,8,64]{1,3,2,0:T(8,128)(2,1)}, bf16[4,512,8,64]{1,3,2,0:T(8,128)(2,1)}, bf16[4,512,8,64]{1,3,2,0:T(8,128)(2,1)}, bf16[4,5...) while((s32[]{:T(128)}, ...), condition=%wide.region_12.13_spmd.clone, body=%wide.region_10.12_spmd.clone.sunk | while | flops 340655104 | bytes 58091296 | solution.py:260
  1189.7 5.9 convolution_convert_fusion.5
  1196.7 5.6 convolution_convert_fusion.2
  1202.4 18.4 reduce-scatter.25.cloned.1.call-done
  1220.8 6.9 convolution_convert_fusion.4
  1227.8 32.1 %reduce-scatter.27.cloned.1.call-done = bf16[128,2048]{1,0:T(8,128)(2,1)} async-done(((bf16[512,2048]{1,0:T(8,128)(2,1)}), bf16[128,2048]{1,0:T(8,128)(2,1)}) %reduce-scatter.27.cloned.1.call-update) | async-done | bytes 524304
  1259.9 6.8 convolution_convert_fusion.3
  1267.9 15.7 convolution_convert_fusion
  1284.6 16.5 convolution_convert_fusion.1
  1301.7 48.1 %reduce-scatter.15.cloned.1.call-done = bf16[512,2048]{1,0:T(8,128)(2,1)} async-done(((bf16[2048,2048]{1,0:T(8,128)(2,1)}), bf16[512,2048]{1,0:T(8,128)(2,1)}) %reduce-scatter.15.cloned.1.call-update) | async-done | bytes 2097168 | tf_op jit(solution)/shard_map/reduce_scatter | solution.py:309
  1349.8 89.8 %reduce-scatter.21.cloned.1.call-done = bf16[512,2048]{1,0:T(8,128)(2,1)} async-done(((bf16[2048,2048]{1,0:T(8,128)(2,1)}), bf16[512,2048]{1,0:T(8,128)(2,1)}) %reduce-scatter.21.cloned.1.call-update) | async-done | bytes 2097168 | tf_op jit(solution)/shard_map/reduce_scatter | solution.py:327
  1439.6 89.9 %reduce-scatter.17.cloned.1.call-done = bf16[512,2048]{1,0:T(8,128)(2,1)} async-done(((bf16[2048,2048]{1,0:T(8,128)(2,1)}), bf16[512,2048]{1,0:T(8,128)(2,1)}) %reduce-scatter.17.cloned.1.call-update) | async-done | bytes 2097168 | tf_op jit(solution)/shard_map/reduce_scatter | solution.py:315
  1529.5 89.8 %reduce-scatter.19.cloned.1.call-done = bf16[512,2048]{1,0:T(8,128)(2,1)} async-done(((bf16[2048,2048]{1,0:T(8,128)(2,1)}), bf16[512,2048]{1,0:T(8,128)(2,1)}) %reduce-scatter.19.cloned.1.call-update) | async-done | bytes 2097168 | tf_op jit(solution)/shard_map/reduce_scatter | solution.py:321
  1619.3 291.6 %reduce-scatter.23.cloned.1.call-done = bf16[2048,2048]{1,0:T(8,128)(2,1)} async-done(((bf16[2048,8192]{1,0:T(8,128)(2,1)}), bf16[2048,2048]{1,0:T(8,128)(2,1)}) %reduce-scatter.23.cloned.1.call-update) | async-done | bytes 8388624 | tf_op jit(solution)/shard_map/reduce_scatter | solution.py:207
  1910.9 291.9 %reduce-scatter.29.cloned.1.call-done = bf16[2048,2048]{1,0:T(8,128)(2,1)} async-done(((bf16[8192,2048]{1,0:T(8,128)(2,1)}), bf16[2048,2048]{1,0:T(8,128)(2,1)}) %reduce-scatter.29.cloned.1.call-update) | async-done | bytes 8388624
  2203.5 8.1 all-gather.7
  2214.0 7.0 fusion.90
  2221.0 17.8 fusion.59
  2238.9 7.4 convolution_add_fusion.3
  2246.3 45.8 %all-gather.31.cloned.1.call-done = bf16[2048,2048]{1,0:T(8,128)(2,1)} async-done(((bf16[512,2048]{1,0:T(8,128)(2,1)}), bf16[2048,2048]{1,0:T(8,128)(2,1)}) %all-gather.31.cloned.1.call-update) | async-done | bytes 8388624 | tf_op jit(solution)/shard_map/all_gather | solution.py:194
  2292.1 6.8 fusion.73
  2298.9 16.1 all-reduce.12
  2315.6 28.0 all-reduce.10
  2350.1 439.9 %all-reduce.15.cloned.1.call-done = (bf16[512,2048]{1,0:T(8,128)(2,1)}, bf16[512,2048]{1,0:T(8,128)(2,1)}, bf16[512,2048]{1,0:T(8,128)(2,1)}, bf16[512,2048]{1,0...) async-done(((bf16[512,2048]{1,0:T(8,128)(2,1)}, bf16[512,2048]{1,0:T(8,128)(2,1)}, bf16[512,2048]{1,0:T(8,128)(2,1)}, bf16[512,2048]{1,0:T(8,128)(2,1)}, ...) | async-done | bytes 25165840 | tf_op jit(solution)/shard_map/psum | solution.py:346
  2801.9 11.7 convert_element_type.296
  2813.6 11.7 convert_element_type.299
  (278 shorter events, 120.8 us)
Async XLA Ops:
  7.2 240.6 %all-gather.21.cloned.1.call-start = ((), (), s32[]{:S(2)}) async-start(), calls=%async_computation.10 | async-start | bytes 10485760 | tf_op jit(solution)/shard_map/all_gather | solution.py:135
  7.9 287.2 %all-gather.17.cloned.1.call-start = ((), (), s32[]{:S(2)}) async-start(), calls=%async_computation.8 | async-start | bytes 2621440 | tf_op jit(solution)/shard_map/all_gather | solution.py:154
  8.0 75.5 %collective-permute-start = (bf16[512,2048]{1,0:T(8,128)(2,1)}, bf16[512,2048]{1,0:T(8,128)(2,1)S(1)}, u32[]{:S(2)}, u32[]{:S(2)}) collective-permute-start(bf16[512,2048]{1,0:T(8,128)(2,1)} %param.31), channel_id=1, source_target_pairs={{0,1},{1,2},{2,3},{3,0},{4,5},{5,6},{6,7},{7,4},{8,9},{9,10},{10,1... | collective-permute-start | bytes 6291464 | tf_op jit(solution)/shard_map/ppermute | solution.py:19
  83.5 153.1 %collective-permute-start.1 = (bf16[512,2048]{1,0:T(8,128)(2,1)S(1)}, bf16[512,2048]{1,0:T(8,128)(2,1)}, u32[]{:S(2)}, u32[]{:S(2)}) collective-permute-start(bf16[512,2048]{1,0:T(8,128)(2,1)S(1)} %collective-permute-done), channel_id=1, source_target_pairs={{0,1},{1,2},{2,3},{3,0},{4,5},{5,6},{6,7},{7,4},{8,9},{9,10},{10,1... | collective-permute-start | bytes 6291464 | tf_op jit(solution)/shard_map/ppermute | solution.py:19
  85.9 153.2 %collective-permute-start.2 = (bf16[512,2048]{1,0:T(8,128)(2,1)}, bf16[512,2048]{1,0:T(8,128)(2,1)}, u32[]{:S(2)}, u32[]{:S(2)}) collective-permute-start(bf16[512,2048]{1,0:T(8,128)(2,1)} %param.31), channel_id=1, source_target_pairs={{0,3},{1,0},{2,1},{3,2},{4,7},{5,4},{6,5},{7,6},{8,11},{9,8},{10,9... | collective-permute-start | bytes 6291464 | tf_op jit(solution)/shard_map/ppermute | solution.py:21
  236.6 2.2 copy-start.3
  242.8 2.0 copy-start
  247.0 125.5 %all-gather.19.cloned.1.call-start = ((), (), s32[]{:S(2)}) async-start(), calls=%async_computation.9 | async-start | bytes 10485760 | tf_op jit(solution)/shard_map/all_gather | solution.py:134
  247.8 162.4 %all-gather.23.cloned.1.call-start = ((), (), s32[]{:S(2)}) async-start(), calls=%async_computation.11 | async-start | bytes 2621440 | tf_op jit(solution)/shard_map/all_gather | solution.py:153
  253.4 246.1 %all-gather.25.cloned.1.call-start = ((), (), s32[]{:S(2)}) async-start(), calls=%async_computation.12 | async-start | bytes 10485760 | tf_op jit(solution)/shard_map/all_gather | solution.py:137
  253.9 544.5 %all-gather.27.cloned.1.call-start = ((), (), s32[]{:S(2)}) async-start(), calls=%async_computation.13 | async-start | bytes 41943040 | tf_op jit(solution)/shard_map/all_gather | solution.py:180
  254.5 9.0 copy-start.24
  254.5 16.7 copy-start.22
  254.6 25.1 copy-start.25
  254.6 32.2 %copy-start.26 = (bf16[512]{0:T(512)(128)(2,1)S(1)}, bf16[512]{0:T(512)(128)(2,1)}, u32[]{:S(2)}) copy-start(bf16[512]{0:T(512)(128)(2,1)} %param.35) | copy-start | bytes 3076
  254.6 40.5 %copy-start.28 = (s32[128]{0:T(128)S(1)}, s32[128]{0:T(128)}, u32[]{:S(2)}) copy-start(s32[128]{0:T(128)} %param.25) | copy-start | bytes 1540
  254.6 842.9 %all-gather.29.cloned.1.call-start = ((), (), s32[]{:S(2)}) async-start(), calls=%async_computation.14 | async-start | bytes 41943040 | tf_op jit(solution)/shard_map/all_gather | solution.py:182
  255.3 965.5 %reduce-scatter.25.cloned.1.call-start = ((), (), s32[]{:S(2)}) async-start(), calls=%async_computation.21 | async-start | bytes 2621440
  1153.0 1.6 copy-start.18
  1153.0 2.4 copy-start.20
  1153.8 3.0 copy-start.8
  1154.9 1.9 copy-start.19
  1160.8 2.4 copy-start.20
  1161.6 3.0 copy-start.8
  1162.7 1.9 copy-start.19
  1168.6 1.6 copy-start.18
  1168.6 2.4 copy-start.20
  1169.4 3.0 copy-start.8
  1170.5 1.9 copy-start.19
  1176.4 2.4 copy-start.20
  1177.2 3.0 copy-start.8
  1178.3 1.9 copy-start.19
  1185.4 4.2 copy-start.9
  1185.5 74.4 %reduce-scatter.27.cloned.1.call-start = ((), (), s32[]{:S(2)}) async-start(), calls=%async_computation.22 | async-start | bytes 2621440
  1189.6 160.2 %reduce-scatter.15.cloned.1.call-start = ((), (), s32[]{:S(2)}) async-start(), calls=%async_computation.16 | async-start | bytes 10485760 | tf_op jit(solution)/shard_map/reduce_scatter | solution.py:309
  1195.6 244.0 %reduce-scatter.21.cloned.1.call-start = ((), (), s32[]{:S(2)}) async-start(), calls=%async_computation.19 | async-start | bytes 10485760 | tf_op jit(solution)/shard_map/reduce_scatter | solution.py:327
  1202.3 327.2 %reduce-scatter.17.cloned.1.call-start = ((), (), s32[]{:S(2)}) async-start(), calls=%async_computation.17 | async-start | bytes 10485760 | tf_op jit(solution)/shard_map/reduce_scatter | solution.py:315
  1227.8 391.5 %reduce-scatter.19.cloned.1.call-start = ((), (), s32[]{:S(2)}) async-start(), calls=%async_computation.18 | async-start | bytes 10485760 | tf_op jit(solution)/shard_map/reduce_scatter | solution.py:321
  1266.7 644.2 %reduce-scatter.23.cloned.1.call-start = ((), (), s32[]{:S(2)}) async-start(), calls=%async_computation.20 | async-start | bytes 41943040 | tf_op jit(solution)/shard_map/reduce_scatter | solution.py:207
  1283.6 919.2 %reduce-scatter.29.cloned.1.call-start = ((), (), s32[]{:S(2)}) async-start(), calls=%async_computation.23 | async-start | bytes 41943040
  1301.1 991.0 %all-gather.31.cloned.1.call-start = ((), (), s32[]{:S(2)}) async-start(), calls=%async_computation.15 | async-start | bytes 10485760 | tf_op jit(solution)/shard_map/all_gather | solution.py:194
  1301.7 1488.3 %all-reduce.15.cloned.1.call-start = ((), (), s32[]{:S(2)}) async-start(), calls=%async_computation.24 | async-start | bytes 50331648 | tf_op jit(solution)/shard_map/psum | solution.py:346
  2202.8 8.8 copy-start.29
  2221.0 17.8 copy-start.10
  2246.3 102.5 %copy-start.13 = (f32[128,2048]{1,0:T(8,128)S(1)}, f32[128,2048]{1,0:T(8,128)}, u32[]{:S(2)}) copy-start(f32[128,2048]{1,0:T(8,128)} %get-tuple-element.224) | copy-start | bytes 3145732
  2790.0 4.3 copy-start.17
  2794.3 2.5 copy-start.16
  2796.8 2.5 copy-start.15
  (26 other events, 30.3 us)
Sparse Core Ops, SparseCore 0:
  9.9 155.4 all-gather.20
  247.1 35.8 all-gather.16
  284.9 87.6 all-gather.18
  374.8 35.3 all-gather.22
  411.8 87.5 all-gather.24
  501.2 297.2 all-gather.26
  800.3 297.2 all-gather.28
  1185.6 35.1 reduce-scatter.24
  1224.6 35.1 reduce-scatter.26
  1263.3 86.3 reduce-scatter.14
  1353.1 86.3 reduce-scatter.20
  1443.1 86.3 reduce-scatter.16
  1532.9 86.4 reduce-scatter.18
  1622.2 288.6 reduce-scatter.22
  1914.1 288.6 reduce-scatter.28
  2204.5 87.5 all-gather.30
  2295.2 494.7 all-reduce.14
